TPU v7x, 32 devices: a whole 2x2x4 slice. The times are simulated.
32 devices in a mesh: dp: 2 (over x), ts: 16 (over z, y, core).
Axes of the slice: x: 2, y: 2, z: 4, core: 2. Of those that a mesh axis runs over, the one named last changes fastest.
Arguments:
- clip_video: bfloat16 [64, 4, 40, 128], P(('dp', 'ts')), may hold values from -6 to 6
- conv_weight: bfloat16 [3, 3, 3, 128, 128], replicated, may hold values from -0.109375 to 0.109375
- embed_weight: bfloat16 [128, 5120], replicated, may hold values from -0.5 to 0.5
- gain_spatial: float32 [5120], replicated, may hold values from 0.5 to 1.5
- gain_temporal: float32 [5120], replicated, may hold values from 0.5 to 1.5
- input_spatial: bfloat16 [5120, 384], P(('dp', 'ts')), may hold values from -0.078125 to 0.078125
- input_temporal: bfloat16 [5120, 384], P(('dp', 'ts')), may hold values from -0.078125 to 0.078125
- output_spatial: bfloat16 [128, 5120], replicated, may hold values from -2 to 2
- output_temporal: bfloat16 [128, 5120], replicated, may hold values from -2 to 2
- cotangent: bfloat16 [64, 4, 40, 5120], P(('dp', 'ts')), may hold values from -6 to 6
Outputs:
- layer_output: bfloat16 [64, 4, 40, 5120], P(('dp', 'ts'))
- grad_spatial: float32 [5120, 384], P(('dp', 'ts'))
All inputs are finite; a program needn't handle non-finite values.
Results may differ from a plain program's by a relative error of at most 0.015.
Values may be sent and summed in bfloat16 or wider, within the bound.
A program may use at most 128 MiB of HBM per device.

v0:
```python
import jax
import jax.numpy as jnp
from jax import lax
from jax.sharding import PartitionSpec as P

FR = 16
epsilon = 1e-06
masked = -1e30
F32 = jnp.float32
BF16 = jnp.bfloat16


def mm(a, b, dims=((1,), (0,))):
    return lax.dot_general(a, b, (dims, ((), ())), preferred_element_type=F32)


def mm_t(a, b):
    return mm(a, b, ((1,), (1,)))


def t_mm(a, b):
    return mm(a, b, ((0,), (0,)))


def wide_mm(a, b):
    high = b.astype(BF16)
    low = (b - high.astype(F32)).astype(BF16)
    return mm(a, high) + mm(a, low)


def conv_local(volume, weight, count):
    frames, height, columns, channels = volume.shape
    padded = jnp.pad(volume, ((0, 0), (1, 1), (1, 1), (0, 0)))
    summed = jnp.zeros((count * height * columns, weight.shape[-1]), F32)
    for a in range(3):
        for b in range(3):
            for e in range(3):
                window = padded[2 - a : 2 - a + count, b : b + height, e : e + columns, :]
                summed = summed + mm(window.reshape(-1, channels), weight[a, b, e])
    return summed


def attend_forward(q, k, v, allowed):
    scores = mm_t(q, k) * q.shape[-1] ** (-0.5)
    scores = jnp.where(allowed, scores, masked)
    raised = jnp.exp(scores - jnp.max(scores, axis=-1, keepdims=True))
    attend = raised / jnp.sum(raised, axis=-1, keepdims=True)
    return (mm(attend.astype(BF16), v).astype(BF16), attend)


def attend_backward(q, k, v, attend, g):
    scale = q.shape[-1] ** (-0.5)
    grad_attend = mm_t(g, v)
    grad_values = t_mm(attend.astype(BF16), g)
    inner = jnp.sum(grad_attend * attend, axis=-1, keepdims=True)
    grad_scores = (attend * (grad_attend - inner)).astype(BF16)
    grad_q = mm(grad_scores, k) * scale
    grad_k = t_mm(grad_scores, q) * scale
    return jnp.concatenate([grad_q, grad_k, grad_values], axis=-1).astype(BF16)


def shards(
    clip_video,
    conv_weight,
    embed_weight,
    gain_spatial,
    gain_temporal,
    input_spatial,
    input_temporal,
    output_spatial,
    output_temporal,
    cotangent,
):
    frames, height, columns, channels = clip_video.shape
    rows, triple = input_spatial.shape
    head = triple // 3
    width = embed_weight.shape[-1]
    places = height * columns
    tokens = frames * places
    ts = lax.axis_size("ts")
    team = FR // frames
    share = places // team
    groups = [[c * team + i for i in range(team)] for c in range(ts // team)]
    me = lax.axis_index("dp") * ts + lax.axis_index("ts")
    route = [(i - 1, i) for i in range(1, ts)]
    prior = lax.ppermute(clip_video, "ts", route)
    volume = jnp.concatenate([prior, clip_video], axis=0)
    basis = jnp.concatenate([embed_weight, output_spatial], axis=0)
    window = lax.dynamic_slice(basis, (0, me * rows), (basis.shape[0], rows)).astype(F32)
    gain_s = lax.dynamic_slice(gain_spatial, (me * rows,), (rows,))
    gain_t = lax.dynamic_slice(gain_temporal, (me * rows,), (rows,))
    embed_rows = (window[:channels] * gain_s).astype(BF16)
    part = jnp.concatenate(
        [mm(embed_rows, input_spatial), mm((window * gain_t).astype(BF16), input_temporal)], axis=0
    )
    mixed = lax.psum(part.astype(BF16), ("dp", "ts"))
    map_space, map_time = (mixed[:channels], mixed[channels:])
    gram = mm_t(basis, basis)
    cotangent_rows = cotangent.reshape(tokens, width)
    grad_mix_time = mm_t(cotangent_rows, output_temporal).astype(BF16)
    grad_direct = mm_t(cotangent_rows, output_spatial)
    features = jax.nn.gelu(conv_local(volume, conv_weight, frames), approximate=True).astype(BF16)
    squares = jnp.sum(
        wide_mm(features, gram[:channels, :channels]) * features.astype(F32), axis=-1, keepdims=True
    )
    factor_one = lax.rsqrt(jnp.maximum(squares, 0.0) / width + epsilon)
    packed_one = (mm(features, map_space) * factor_one).astype(BF16)
    place = jnp.arange(tokens)
    same_frame = place[:, None] // places == place[None, :] // places
    q, k, v = (packed_one[:, :head], packed_one[:, head : 2 * head], packed_one[:, 2 * head :])
    mixture_one, attend_one = attend_forward(q, k, v, same_frame)
    joint = jnp.concatenate([features, mixture_one], axis=-1)
    spread = wide_mm(joint, gram)
    squares = jnp.sum(spread * joint.astype(F32), axis=-1, keepdims=True)
    factor_two = lax.rsqrt(jnp.maximum(squares, 0.0) / width + epsilon)
    packed_two = (mm(joint, map_time) * factor_two).astype(BF16)
    sent = jnp.concatenate([packed_two, grad_mix_time], axis=-1).reshape(frames, places, 4 * head)
    got = lax.all_to_all(
        sent, "ts", split_axis=1, concat_axis=0, tiled=True, axis_index_groups=groups
    ).reshape(FR * share, 4 * head)
    spot = jnp.arange(FR * share)
    allowed = (spot[:, None] % share == spot[None, :] % share) & (spot[:, None] >= spot[None, :])
    tq, tk, tv, tg = (got[:, i * head : (i + 1) * head] for i in range(4))
    mixture_two, attend_two = attend_forward(tq, tk, tv, allowed)
    grad_two = attend_backward(tq, tk, tv, attend_two, tg)
    back = jnp.concatenate([mixture_two, grad_two], axis=-1).reshape(FR, share, 4 * head)
    home = lax.all_to_all(
        back, "ts", split_axis=0, concat_axis=1, tiled=True, axis_index_groups=groups
    ).reshape(tokens, 4 * head)
    mixture_two, grad_two = (home[:, :head], home[:, head:])
    output = mm(
        jnp.concatenate([joint, mixture_two], axis=-1),
        jnp.concatenate([basis, output_temporal], axis=0),
    ).astype(BF16)
    inner = jnp.sum(grad_two.astype(F32) * packed_two.astype(F32), axis=-1, keepdims=True)
    grad_mix_one = (
        grad_direct
        + factor_two * mm_t(grad_two, map_time[channels:])
        - factor_two**2 * inner / width * spread[:, channels:]
    ).astype(BF16)
    grad_one = attend_backward(q, k, v, attend_one, grad_mix_one)
    scaled = (features.astype(F32) * factor_one).astype(BF16)
    core = lax.psum(t_mm(scaled, grad_one).astype(BF16), ("dp", "ts"))
    return (output.reshape(frames, height, columns, width), t_mm(embed_rows, core))


def solution(mesh):
    placed = (
        P(("dp", "ts"), None, None, None),
        P(),
        P(),
        P(),
        P(),
        P(("dp", "ts"), None),
        P(("dp", "ts"), None),
        P(),
        P(),
        P(("dp", "ts"), None, None, None),
    )
    return jax.shard_map(
        shards,
        mesh=mesh,
        in_specs=placed,
        out_specs=(P(("dp", "ts"), None, None, None), P(("dp", "ts"), None)),
        check_vma=False,
    )
```

profile of v0, /device:TPU:8, one launch (start us, length us, event | category | flops | bytes accessed | tf_op | source)
XLA Modules:
  0.0 330.4 jit_solution(1640951019662262618)
XLA Ops:
  7.2 2.2 collective-permute-start
  9.4 2.5 constant_dynamic-update-slice_fusion.3
  11.9 2.5 constant_dynamic-update-slice_fusion.2
  17.0 1.2 convolution_convert_fusion.1
  18.2 1.1 convolution_convert_fusion.3
  20.1 3.5 %fusion.148 = f32[256,256]{1,0:T(8,128)S(1)} fusion(bf16[256,5120]{1,0:T(8,128)(2,1)} %constant_dynamic-update-slice_fusion.2), kind=kOutput, calls=%fused_computation.247 | convolution fusion | flops 671088640 | bytes 2883584 | tf_op jit(solution)/shard_map/dot_general | solution.py:14
  30.7 120.0 %all-reduce.4.cloned.1.call-done = bf16[384,384]{1,0:T(8,128)(2,1)} async-done(((bf16[384,384]{1,0:T(8,128)(2,1)}), bf16[384,384]{1,0:T(8,128)(2,1)}) %all-reduce.4.cloned.1.call-update) | async-done | bytes 294928 | tf_op jit(solution)/shard_map/psum | solution.py:96
  150.8 1.1 fusion.7
  155.4 1.0 copy.12
  156.5 4.2 %all-to-all-start = ((bf16[2,160,512]{2,0,1:T(2,128)(2,1)}), bf16[2,160,512]{2,0,1:T(2,128)(2,1)}, u32[]{:S(2)}, u32[]{:S(2)}) async-start(bf16[2,160,512]{2,0,1:T(2,128)(2,1)} %copy.12), calls=%async_computation | async-start | bytes 655360 | tf_op jit(solution)/shard_map/all_to_all | solution.py:118
  160.7 6.2 %all-to-all-done = bf16[2,160,512]{2,0,1:T(2,128)(2,1)} async-done(((bf16[2,160,512]{2,0,1:T(2,128)(2,1)}), bf16[2,160,512]{2,0,1:T(2,128)(2,1)}, u32[]{:S(2)}, u32[]{:S(2)}) %all-to-all-start) | async-done | bytes 327712 | tf_op jit(solution)/shard_map/all_to_all | solution.py:118
  166.9 1.8 copy.13
  168.7 1.8 reshape.248
  170.5 1.2 fusion.147
  171.8 1.2 convolution_convert_fusion.7
  174.9 1.8 reshape.249
  176.7 10.8 %all_to_all.30 = bf16[16,20,512]{2,1,0:T(8,128)(2,1)S(1)} all-to-all(bf16[16,20,512]{2,1,0:T(8,128)(2,1)} %reshape.249), channel_id=1, replica_groups={{0,1,2,3,4,5,6,7},{8,9,10,11,12,13,14,15},{16,17,18,19,20,21,22,23},{24..., dimensions={0} | all-to-all | bytes 655360 | tf_op jit(solution)/shard_map/all_to_all | solution.py:127
  188.7 1.8 reshape.250
  190.5 1.2 multiply_reduce_fusion.1
  191.7 1.3 convolution_multiply_fusion.6
  193.0 2.4 fusion.16
  197.7 5.7 %convolution_convert_fusion = bf16[320,5120]{1,0:T(8,128)(2,1)} fusion(bf16[128,5120]{1,0:T(8,128)(2,1)} %param.18, bf16[128,5120]{1,0:T(8,128)(2,1)} %param.17, bf16[128,5120]{1,0:T(8,128)(2,1)} %param.12, bf16[320,128]{1,0:T(8,128)(2,1)S(1)} %slice-done, bf16[320,128]{1,0:T(8,128)(2,1)S(1)} %convolution_convert_fusion.8, bf16[320,128]{1,0:T(8,128)(2,1)S(1)} %fusion.43), kind=kOutput, calls=%fused_computation | convolution fusion | flops 1272463360 | bytes 7454720 | tf_op jit(solution)/shard_map/dot_general | solution.py:14
  203.3 118.4 %all-reduce.6.cloned.1.call-done = bf16[128,384]{1,0:T(8,128)(2,1)} async-done(((bf16[128,384]{1,0:T(8,128)(2,1)}), bf16[128,384]{1,0:T(8,128)(2,1)}) %all-reduce.6.cloned.1.call-update) | async-done | bytes 98320 | tf_op jit(solution)/shard_map/psum | solution.py:143
  321.7 1.9 fusion.129
  (102 shorter events, 19.2 us)
Async XLA Ops:
  7.2 16.5 %copy-start = (bf16[2,4,40,5120]{3,2,1,0:T(8,128)(2,1)S(1)}, bf16[2,4,40,5120]{3,2,1,0:T(8,128)(2,1)}, u32[]{:S(2)}) copy-start(bf16[2,4,40,5120]{3,2,1,0:T(8,128)(2,1)} %param.19) | copy-start | bytes 9830404
  7.2 143.6 %all-reduce.4.cloned.1.call-start = ((), (), s32[]{:S(2)}) async-start(), calls=%async_computation.2 | async-start | bytes 589824 | tf_op jit(solution)/shard_map/psum | solution.py:96
  7.2 17.5 %collective-permute-start = (bf16[2,4,40,128]{3,2,1,0:T(8,128)(2,1)}, bf16[2,4,40,128]{3,2,1,0:T(8,128)(2,1)S(1)}, u32[]{:S(2)}, u32[]{:S(2)}) collective-permute-start(bf16[2,4,40,128]{3,2,1,0:T(8,128)(2,1)} %param.10), channel_id=1, source_target_pairs={{0,1},{1,2},{2,3},{3,4},{4,5},{5,6},{6,7},{7,8},{8,9},{9,10},{10,1... | collective-permute-start | bytes 245768 | tf_op jit(solution)/shard_map/ppermute | solution.py:86
  9.4 7.6 %copy-start.13 = (bf16[160,384]{1,0:T(8,128)(2,1)S(1)}, bf16[160,384]{1,0:T(8,128)(2,1)}, u32[]{:S(2)}) copy-start(bf16[160,384]{1,0:T(8,128)(2,1)} %param.16) | copy-start | bytes 368644
  15.4 2.8 copy-start.6
  20.1 3.6 %copy-start.5 = (bf16[128,5120]{1,0:T(8,128)(2,1)S(1)}, bf16[128,5120]{1,0:T(8,128)(2,1)}, u32[]{:S(2)}) copy-start(bf16[128,5120]{1,0:T(8,128)(2,1)} %param.18) | copy-start | bytes 3932164
  23.6 6.8 %copy-start.3 = (f32[256,256]{1,0:T(8,128)}, f32[256,256]{1,0:T(8,128)S(1)}, u32[]{:S(2)}) copy-start(f32[256,256]{1,0:T(8,128)S(1)} %fusion.148) | copy-start | bytes 786436
  23.7 1.1 copy-start.12
  24.7 1.2 copy-start.8
  150.7 2.5 copy-start.4
  151.9 1.3 copy-start.10
  151.9 2.5 copy-start.14
  152.2 0.8 copy-start.1
  154.7 0.7 copy-start.7
  156.5 10.4 %all-to-all-start = ((bf16[2,160,512]{2,0,1:T(2,128)(2,1)}), bf16[2,160,512]{2,0,1:T(2,128)(2,1)}, u32[]{:S(2)}, u32[]{:S(2)}) async-start(bf16[2,160,512]{2,0,1:T(2,128)(2,1)} %copy.12), calls=%async_computation | async-start | bytes 655360 | tf_op jit(solution)/shard_map/all_to_all | solution.py:118
  160.7 161.0 %all-reduce.6.cloned.1.call-start = ((), (), s32[]{:S(2)}) async-start(), calls=%async_computation.3 | async-start | bytes 196608 | tf_op jit(solution)/shard_map/psum | solution.py:143
  170.5 2.5 copy-start.9
  193.0 2.4 copy-start.2
  193.0 2.4 copy-start.11
  195.7 1.9 slice-start
Sparse Core Ops, SparseCore 0:
  20.2 130.4 all-reduce.3
  197.8 123.8 all-reduce.5
where the time goes:
time: 331 us; the launch traced here: 330 us
  waiting for transfers between devices  245 us (74%)
  matrix products  31.3 us (9%)
  local copies, waits for them, and re-layouts  18.4 us (6%)
  between operations  14.5 us (4%)
  blocking collectives  10.8 us (3%)
  starting transfers between devices  6.42 us (2%)
  other arithmetic  4.29 us (1%)
    psum x1, waiting for transfers between devices, shards(): mixed = lax.psum(part.astype(BF16), ('dp', 'ts'))  120 us
    psum x1, waiting for transfers between devices, shards(): core = lax.psum(t_mm(scaled, grad_one).astype(BF16), ('dp', 'ts'))  118 us
    dot_general x54, matrix products, mm(): return lax.dot_general(a, b, (dims, ((), ())), preferred_element_type=F32)  31.3 us
    all_to_all x1, blocking collectives, shards(): lax.all_to_all(back, 'ts', split_axis=0, concat_axis=1, tiled=True, axis_...  10.8 us
  transfers between devices with their start and end apart: 4, of which 3 were waited for; matrix products, arithmetic and copies ran while one was open for 8% of the time, Pallas kernels for 0%

commit v1 on v0

--- a/solution.py
+++ b/solution.py
@@ -140,7 +140,7 @@
     ).astype(BF16)
     grad_one = attend_backward(q, k, v, attend_one, grad_mix_one)
     scaled = (features.astype(F32) * factor_one).astype(BF16)
-    core = lax.psum(t_mm(scaled, grad_one).astype(BF16), ("dp", "ts"))
+    core = jnp.sum(lax.all_gather(t_mm(scaled, grad_one).astype(BF16), ("dp", "ts")), axis=0)
     return (output.reshape(frames, height, columns, width), t_mm(embed_rows, core))
 
 

time: 331 us -> 271 us (0.82); the launches traced: 330 us -> 267 us
  waiting for transfers between devices: 245 us -> 178 us
    psum x1 -> x0, waiting for transfers between devices: 118 us -> none  [shards(): core = lax.psum(t_mm(scaled, grad_one).astype(BF16), ('dp', 'ts'))]
    all_gather x0 -> x1, waiting for transfers between devices: none -> 51.9 us  [shards(): lax.all_gather(t_mm(scaled, grad_one).astype(BF16), ('dp', 'ts'))]
  transfers between devices with their start and end apart: 4 -> 4, of which waited for: 3 -> 3; matrix products, arithmetic and copies ran while one was open for 8% -> 10% of each run, Pallas kernels for 0% -> 0%
where the time goes in v1:
time: 271 us; the launch traced here: 267 us
  waiting for transfers between devices  178 us (66%)
  matrix products  31.2 us (12%)
  local copies, waits for them, and re-layouts  18.5 us (7%)
  between operations  14.5 us (5%)
  blocking collectives  10.8 us (4%)
  other arithmetic  7.26 us (3%)
  starting transfers between devices  6.41 us (2%)
    psum x1, waiting for transfers between devices, shards(): mixed = lax.psum(part.astype(BF16), ('dp', 'ts'))  120 us
    all_gather x1, waiting for transfers between devices, shards(): lax.all_gather(t_mm(scaled, grad_one).astype(BF16), ('dp', 'ts'))  51.9 us
    dot_general x54, matrix products, mm(): return lax.dot_general(a, b, (dims, ((), ())), preferred_element_type=F32)  31.2 us
    all_to_all x1, blocking collectives, shards(): lax.all_to_all(back, 'ts', split_axis=0, concat_axis=1, tiled=True, axis_...  10.8 us
    all_to_all x1, waiting for transfers between devices, shards(): lax.all_to_all(sent, 'ts', split_axis=1, concat_axis=0, tiled=True, axis_...  6.24 us
  transfers between devices with their start and end apart: 4, of which 3 were waited for; matrix products, arithmetic and copies ran while one was open for 10% of the time, Pallas kernels for 0%

profile of v1, /device:TPU:8, one launch (start us, length us, event | category | flops | bytes accessed | tf_op | source)
XLA Modules:
  0.0 266.9 jit_solution(2848588338631703226)
XLA Ops:
  7.2 2.2 collective-permute-start
  9.4 2.5 constant_dynamic-update-slice_fusion.3
  11.9 2.5 constant_dynamic-update-slice_fusion.2
  17.0 1.2 convolution_convert_fusion.1
  18.2 1.1 convolution_convert_fusion.3
  20.1 3.5 %fusion.148 = f32[256,256]{1,0:T(8,128)S(1)} fusion(bf16[256,5120]{1,0:T(8,128)(2,1)} %constant_dynamic-update-slice_fusion.2), kind=kOutput, calls=%fused_computation.247 | convolution fusion | flops 671088640 | bytes 2883584 | tf_op jit(solution)/shard_map/dot_general | solution.py:14
  30.7 120.1 %all-reduce.3.cloned.1.call-done = bf16[384,384]{1,0:T(8,128)(2,1)} async-done(((bf16[384,384]{1,0:T(8,128)(2,1)}), bf16[384,384]{1,0:T(8,128)(2,1)}) %all-reduce.3.cloned.1.call-update) | async-done | bytes 294928 | tf_op jit(solution)/shard_map/psum | solution.py:96
  150.8 1.1 fusion.7
  156.5 4.2 %all-to-all-start = ((bf16[2,160,512]{2,0,1:T(2,128)(2,1)}), bf16[2,160,512]{2,0,1:T(2,128)(2,1)}, u32[]{:S(2)}, u32[]{:S(2)}) async-start(bf16[2,160,512]{2,0,1:T(2,128)(2,1)} %copy.12), calls=%async_computation | async-start | bytes 655360 | tf_op jit(solution)/shard_map/all_to_all | solution.py:118
  160.7 6.2 %all-to-all-done = bf16[2,160,512]{2,0,1:T(2,128)(2,1)} async-done(((bf16[2,160,512]{2,0,1:T(2,128)(2,1)}), bf16[2,160,512]{2,0,1:T(2,128)(2,1)}, u32[]{:S(2)}, u32[]{:S(2)}) %all-to-all-start) | async-done | bytes 327712 | tf_op jit(solution)/shard_map/all_to_all | solution.py:118
  166.9 1.8 copy.13
  168.7 1.8 reshape.248
  170.5 1.2 fusion.147
  171.8 1.2 convolution_convert_fusion.7
  174.9 1.8 reshape.249
  176.7 10.8 %all_to_all.30 = bf16[16,20,512]{2,1,0:T(8,128)(2,1)S(1)} all-to-all(bf16[16,20,512]{2,1,0:T(8,128)(2,1)} %reshape.249), channel_id=1, replica_groups={{0,1,2,3,4,5,6,7},{8,9,10,11,12,13,14,15},{16,17,18,19,20,21,22,23},{24..., dimensions={0} | all-to-all | bytes 655360 | tf_op jit(solution)/shard_map/all_to_all | solution.py:127
  188.8 1.8 reshape.250
  190.6 1.2 multiply_reduce_fusion.1
  191.8 1.3 convolution_multiply_fusion.6
  193.1 2.4 fusion.16
  197.7 5.7 %convolution_convert_fusion = bf16[320,5120]{1,0:T(8,128)(2,1)} fusion(bf16[128,5120]{1,0:T(8,128)(2,1)} %param.18, bf16[128,5120]{1,0:T(8,128)(2,1)} %param.17, bf16[128,5120]{1,0:T(8,128)(2,1)} %param.12, bf16[320,128]{1,0:T(8,128)(2,1)S(1)} %slice-done, bf16[320,128]{1,0:T(8,128)(2,1)S(1)} %convolution_convert_fusion.8, bf16[320,128]{1,0:T(8,128)(2,1)S(1)} %fusion.43), kind=kOutput, calls=%fused_computation | convolution fusion | flops 1272463360 | bytes 7454720 | tf_op jit(solution)/shard_map/dot_general | solution.py:14
  203.4 51.9 %all-gather.3.cloned.1.call-done = bf16[4096,384]{1,0:T(8,128)(2,1)} async-done(((bf16[128,384]{1,0:T(8,128)(2,1)}), bf16[4096,384]{1,0:T(8,128)(2,1)}) %all-gather.3.cloned.1.call-update) | async-done | bytes 3145744 | tf_op jit(solution)/shard_map/all_gather | solution.py:143
  255.3 3.0 %reduce_sum.82 = bf16[128,384]{1,0:T(8,128)(2,1)} reduce(bf16[32,128,384]{2,1,0:T(8,128)(2,1)} %bitcast.166, bf16[]{:T(256)} %constant.28.clone.1), dimensions={0}, to_apply=%region_10.11 | reduce | flops 1523712 | bytes 3244034 | tf_op jit(solution)/shard_map/reduce_sum | solution.py:143
  258.3 1.8 fusion.129
  (105 shorter events, 20.3 us)
Async XLA Ops:
  7.2 16.4 %copy-start = (bf16[2,4,40,5120]{3,2,1,0:T(8,128)(2,1)S(1)}, bf16[2,4,40,5120]{3,2,1,0:T(8,128)(2,1)}, u32[]{:S(2)}) copy-start(bf16[2,4,40,5120]{3,2,1,0:T(8,128)(2,1)} %param.19) | copy-start | bytes 9830404
  7.2 143.6 %all-reduce.3.cloned.1.call-start = ((), (), s32[]{:S(2)}) async-start(), calls=%async_computation.2 | async-start | bytes 589824 | tf_op jit(solution)/shard_map/psum | solution.py:96
  7.2 17.5 %collective-permute-start = (bf16[2,4,40,128]{3,2,1,0:T(8,128)(2,1)}, bf16[2,4,40,128]{3,2,1,0:T(8,128)(2,1)S(1)}, u32[]{:S(2)}, u32[]{:S(2)}) collective-permute-start(bf16[2,4,40,128]{3,2,1,0:T(8,128)(2,1)} %param.10), channel_id=1, source_target_pairs={{0,1},{1,2},{2,3},{3,4},{4,5},{5,6},{6,7},{7,8},{8,9},{9,10},{10,1... | collective-permute-start | bytes 245768 | tf_op jit(solution)/shard_map/ppermute | solution.py:86
  9.4 7.6 %copy-start.14 = (bf16[160,384]{1,0:T(8,128)(2,1)S(1)}, bf16[160,384]{1,0:T(8,128)(2,1)}, u32[]{:S(2)}) copy-start(bf16[160,384]{1,0:T(8,128)(2,1)} %param.16) | copy-start | bytes 368644
  15.4 2.8 %copy-start.6 = (f32[256,160]{1,0:T(8,128)}, f32[256,160]{1,0:T(8,128)S(1)}, u32[]{:S(2)}) copy-start(f32[256,160]{1,0:T(8,128)S(1)} %dynamic-slice_convert_fusion) | copy-start | bytes 491524
  20.1 3.6 %copy-start.5 = (bf16[128,5120]{1,0:T(8,128)(2,1)S(1)}, bf16[128,5120]{1,0:T(8,128)(2,1)}, u32[]{:S(2)}) copy-start(bf16[128,5120]{1,0:T(8,128)(2,1)} %param.18) | copy-start | bytes 3932164
  23.6 6.8 %copy-start.3 = (f32[256,256]{1,0:T(8,128)}, f32[256,256]{1,0:T(8,128)S(1)}, u32[]{:S(2)}) copy-start(f32[256,256]{1,0:T(8,128)S(1)} %fusion.148) | copy-start | bytes 786436
  23.6 1.1 copy-start.13
  24.7 1.2 copy-start.9
  150.8 2.5 copy-start.4
  151.9 1.3 copy-start.11
  151.9 2.5 copy-start.15
  152.2 0.8 copy-start.1
  154.7 0.7 copy-start.8
  156.5 10.4 %all-to-all-start = ((bf16[2,160,512]{2,0,1:T(2,128)(2,1)}), bf16[2,160,512]{2,0,1:T(2,128)(2,1)}, u32[]{:S(2)}, u32[]{:S(2)}) async-start(bf16[2,160,512]{2,0,1:T(2,128)(2,1)} %copy.12), calls=%async_computation | async-start | bytes 655360 | tf_op jit(solution)/shard_map/all_to_all | solution.py:118
  160.7 94.6 %all-gather.3.cloned.1.call-start = ((), (), s32[]{:S(2)}) async-start(), calls=%async_computation.3 | async-start | bytes 3244032 | tf_op jit(solution)/shard_map/all_gather | solution.py:143
  170.5 2.5 copy-start.10
  193.1 2.4 copy-start.2
  193.1 2.4 copy-start.12
  195.8 1.9 slice-start
  203.4 54.9 %copy-start.7 = (f32[256,160]{1,0:T(8,128)S(1)}, f32[256,160]{1,0:T(8,128)}, u32[]{:S(2)}) copy-start(f32[256,160]{1,0:T(8,128)} %copy-done.6) | copy-start | bytes 491524
Sparse Core Ops, SparseCore 0:
  20.2 130.5 all-reduce.2
  197.8 57.4 all-gather.2
